TPU v7x, 32 devices: a whole 2x2x4 slice. The times are simulated.
32 devices in a mesh: dp: 8 (over y, x, core), tensor: 4 (over z).
Axes of the slice: x: 2, y: 2, z: 4, core: 2. Of those that a mesh axis runs over, the one named last changes fastest.
Arguments:
- clip_rows: bfloat16 [12544, 1024], P(('dp', 'tensor')), may hold values from -6 to 6
- out_grad: bfloat16 [12544, 1024], P(('dp', 'tensor')), may hold values from -6 to 6
- clip_valid: int32 [8], P('dp'), may hold values from 0 to 1, as said below
- gain_rows: bfloat16 [2, 1024], P(None, ('dp', 'tensor')), may hold values from 0.099609375 to 1.8984375
- bias_rows: bfloat16 [4, 1024], P(None, ('dp', 'tensor')), may hold values from -1.796875 to 1.796875
- qkv_weight: bfloat16 [3, 1024, 1024], P(None, 'dp', 'tensor'), may hold values from -0.1875 to 0.1875
- qv_bias: bfloat16 [2, 16, 64], P(None, 'tensor', 'dp'), may hold values from -3 to 3
- proj_weight: bfloat16 [1024, 1024], P('tensor', 'dp'), may hold values from -4 to 4
- fc1_weight: bfloat16 [1024, 4096], P('dp', 'tensor'), may hold values from -0.1875 to 0.1875
- fc1_bias: bfloat16 [4, 1024], P('tensor', 'dp'), may hold values from -1.796875 to 1.796875
- fc2_weight: bfloat16 [4096, 1024], P('tensor', 'dp'), may hold values from -0.125 to 0.125
Outputs:
- layer_out: bfloat16 [12544, 1024], P(('dp', 'tensor'))
- input_grad: float32 [12544, 1024], P(('dp', 'tensor'))
- grad_gains: float32 [2, 1024], P(None, ('dp', 'tensor'))
- grad_biases: float32 [4, 1024], P(None, ('dp', 'tensor'))
- grad_qkv: float32 [3, 1024, 1024], P(None, 'dp', 'tensor')
- grad_qv_bias: float32 [2, 16, 64], P(None, 'tensor', 'dp')
- grad_proj: float32 [1024, 1024], P('tensor', 'dp')
- grad_fc1: float32 [1024, 4096], P('dp', 'tensor')
- grad_fc1_bias: float32 [4, 1024], P('tensor', 'dp')
- grad_fc2: float32 [4096, 1024], P('tensor', 'dp')
- grad_fc2_bias: float32 [1024], P(('dp', 'tensor'))
Inputs may be any that keep to these rules, and one draw needn't show every extreme that they name: `clip_valid`: exactly 2 of the 8 slots hold a clip; which ones is drawn from the seed.
All inputs are finite; a program needn't handle non-finite values.
Results may differ from a plain program's by a relative error of at most 0.012.
Values may be sent and summed in bfloat16 or wider, within the bound.
No kernel may reach another device: no remote copies, remote signals or barrier semaphores. Data moves between devices by JAX's collectives and lax.ppermute only.
A program may use at most 256 MiB of HBM per device.

v0:
```python
import math
import jax
import jax.numpy as jnp
from jax import lax
from jax.sharding import PartitionSpec as P

HD = 64
norm_eps = 1e-06
root_half = 0.7071067811865476
inv_root_tau = 0.3989422804014327


def normalize(values, gain_row, shift_row):
    centre = jnp.mean(values, axis=1, keepdims=True)
    offsets = values - centre
    inverse = lax.rsqrt(jnp.mean(offsets * offsets, axis=1, keepdims=True) + norm_eps)
    scaled = offsets * inverse
    return (scaled * gain_row + shift_row, scaled, inverse)


def normalize_back(upstream, scaled, inverse, gain_row):
    grad_hat = upstream * gain_row
    return (
        grad_hat
        - jnp.mean(grad_hat, axis=1, keepdims=True)
        - scaled * jnp.mean(grad_hat * scaled, axis=1, keepdims=True)
    ) * inverse


def gelu_value(inputs):
    return 0.5 * inputs * (1.0 + lax.erf(inputs * root_half))


def gelu_slope(inputs):
    return (
        0.5 * (1.0 + lax.erf(inputs * root_half))
        + inputs * jnp.exp(-0.5 * inputs * inputs) * inv_root_tau
    )


def fetch(qkv_weight, proj_weight, fc1_weight, fc2_weight, qv_bias, fc1_bias, gain_rows, bias_rows):
    matrices = (
        lax.all_gather(qkv_weight, "dp", axis=1, tiled=True),
        lax.all_gather(proj_weight, "dp", axis=1, tiled=True),
        lax.all_gather(fc1_weight, "dp", axis=0, tiled=True),
        lax.all_gather(fc2_weight, "dp", axis=1, tiled=True),
        lax.all_gather(qv_bias, "dp", axis=2, tiled=True),
        lax.all_gather(fc1_bias, "dp", axis=1, tiled=True),
    )
    vectors = (
        lax.all_gather(gain_rows, ("dp", "tensor"), axis=1, tiled=True),
        lax.all_gather(bias_rows, ("dp", "tensor"), axis=1, tiled=True),
    )
    return (matrices, (vectors[0].astype(jnp.float32), vectors[1].astype(jnp.float32)))


def spread_rows(local_rows):
    return lax.all_gather(local_rows, "tensor", axis=0, tiled=True)


def reduce_rows(term_fn, row_count):
    return lax.psum_scatter(
        term_fn(jnp.int32(0), lax.axis_size("tensor") * row_count),
        "tensor",
        scatter_dimension=0,
        tiled=True,
    )


def spread_grads(local_rows):
    return lax.all_gather(local_rows, "tensor", axis=0, tiled=True)


def reduce_grads(term_fn, row_count):
    return lax.psum_scatter(
        term_fn(jnp.int32(0), lax.axis_size("tensor") * row_count),
        "tensor",
        scatter_dimension=0,
        tiled=True,
    )


def forward(clip_rows, matrices, vectors):
    w_qkv, w_proj, w_fc1, w_fc2, b_qv, b_fc1 = matrices
    gain_rows, bias_rows = vectors
    row_count = clip_rows.shape[0]
    head_cols = w_qkv.shape[2]
    heads_here = head_cols // HD
    score_scale = 1.0 / math.sqrt(HD)
    inputs = clip_rows.astype(jnp.float32)
    normed_one, scaled_one, inverse_one = normalize(inputs, gain_rows[0], bias_rows[0])
    whole_one = spread_rows(normed_one.astype(jnp.bfloat16))
    seq_len = whole_one.shape[0]
    projected = jnp.einsum("sd,jde->jse", whole_one, w_qkv, preferred_element_type=jnp.float32)
    bias_cols = b_qv.reshape(2, head_cols).astype(jnp.float32)
    queries = (projected[0] + bias_cols[0]).astype(jnp.bfloat16).reshape(seq_len, heads_here, HD)
    keys_all = projected[1].astype(jnp.bfloat16).reshape(seq_len, heads_here, HD)
    values_all = (projected[2] + bias_cols[1]).astype(jnp.bfloat16).reshape(seq_len, heads_here, HD)
    scores = (
        jnp.einsum("qhd,khd->hqk", queries, keys_all, preferred_element_type=jnp.float32)
        * score_scale
    )
    top_score = jnp.max(scores, axis=2, keepdims=True)
    weights_exp = jnp.exp(scores - top_score)
    totals = jnp.sum(weights_exp, axis=2, keepdims=True)
    attn_probs = (weights_exp / totals).astype(jnp.bfloat16)
    log_total = top_score + jnp.log(totals)
    attended = (
        jnp.einsum("hqk,khd->qhd", attn_probs, values_all, preferred_element_type=jnp.float32)
        .reshape(seq_len, head_cols)
        .astype(jnp.bfloat16)
    )

    def proj_term(offset, length):
        return jnp.dot(attended, w_proj, preferred_element_type=jnp.float32)

    residual_one = inputs + (reduce_rows(proj_term, row_count) + bias_rows[2])
    normed_two, scaled_two, inverse_two = normalize(residual_one, gain_rows[1], bias_rows[1])
    whole_two = spread_rows(normed_two.astype(jnp.bfloat16))
    pre_act = jnp.dot(whole_two, w_fc1, preferred_element_type=jnp.float32) + b_fc1.reshape(
        -1
    ).astype(jnp.float32)
    hidden = gelu_value(pre_act).astype(jnp.bfloat16)

    def fc2_term(offset, length):
        return jnp.dot(hidden, w_fc2, preferred_element_type=jnp.float32)

    layer_out = residual_one + (reduce_rows(fc2_term, row_count) + bias_rows[3])
    stored = (
        scaled_one,
        inverse_one,
        whole_one,
        queries,
        keys_all,
        values_all,
        log_total,
        attended,
        scaled_two,
        inverse_two,
        whole_two,
        pre_act,
        hidden,
    )
    return (layer_out, stored)


def backward(upstream, matrices, vectors, stored):
    w_qkv, w_proj, w_fc1, w_fc2, b_qv, b_fc1 = matrices
    gain_rows, bias_rows = vectors
    (
        scaled_one,
        inverse_one,
        whole_one,
        queries,
        keys_all,
        values_all,
        log_total,
        attended,
        scaled_two,
        inverse_two,
        whole_two,
        pre_act,
        hidden,
    ) = stored
    row_count = upstream.shape[0]
    seq_len = queries.shape[0]
    heads_here = queries.shape[1]
    head_cols = heads_here * HD
    score_scale = 1.0 / math.sqrt(HD)
    grad_mlp = upstream.astype(jnp.bfloat16)
    grad_fc2_bias = jnp.sum(grad_mlp.astype(jnp.float32), axis=0)
    whole_mlp = spread_grads(grad_mlp)
    grad_fc2 = jnp.einsum("sf,sd->fd", hidden, whole_mlp, preferred_element_type=jnp.float32)
    grad_hidden = jnp.einsum("sd,fd->sf", whole_mlp, w_fc2, preferred_element_type=jnp.float32)
    grad_pre = (grad_hidden * gelu_slope(pre_act)).astype(jnp.bfloat16)
    grad_fc1_bias = jnp.sum(grad_pre.astype(jnp.float32), axis=0)
    grad_fc1 = jnp.einsum("sd,sf->df", whole_two, grad_pre, preferred_element_type=jnp.float32)

    def fc1_back(offset, length):
        return jnp.einsum("sf,df->sd", grad_pre, w_fc1, preferred_element_type=jnp.float32)

    grad_normed_two = reduce_grads(fc1_back, row_count)
    grad_residual = upstream + normalize_back(
        grad_normed_two, scaled_two, inverse_two, gain_rows[1]
    )
    grad_branch = grad_residual.astype(jnp.bfloat16)
    grad_proj_bias = jnp.sum(grad_branch.astype(jnp.float32), axis=0)
    whole_branch = spread_grads(grad_branch)
    grad_proj = jnp.einsum("se,sd->ed", attended, whole_branch, preferred_element_type=jnp.float32)
    grad_att = (
        jnp.einsum("sd,ed->se", whole_branch, w_proj, preferred_element_type=jnp.float32)
        .astype(jnp.bfloat16)
        .reshape(seq_len, heads_here, HD)
    )
    scores = (
        jnp.einsum("qhd,khd->hqk", queries, keys_all, preferred_element_type=jnp.float32)
        * score_scale
    )
    attn_probs = jnp.exp(scores - log_total)
    grad_probs = jnp.einsum(
        "qhd,khd->hqk", grad_att, values_all, preferred_element_type=jnp.float32
    )
    row_dot = jnp.sum(attn_probs * grad_probs, axis=2, keepdims=True)
    grad_scores = (attn_probs * (grad_probs - row_dot)).astype(jnp.bfloat16)
    grad_query = (
        jnp.einsum("hqk,khd->qhd", grad_scores, keys_all, preferred_element_type=jnp.float32)
        * score_scale
    ).astype(jnp.bfloat16)
    grad_key = (
        jnp.einsum("hqk,qhd->khd", grad_scores, queries, preferred_element_type=jnp.float32)
        * score_scale
    ).astype(jnp.bfloat16)
    grad_value = jnp.einsum(
        "hqk,qhd->khd",
        attn_probs.astype(jnp.bfloat16),
        grad_att,
        preferred_element_type=jnp.float32,
    ).astype(jnp.bfloat16)
    grad_qkv = jnp.stack([grad_query, grad_key, grad_value]).reshape(3, seq_len, head_cols)
    grad_qv = jnp.stack(
        [
            jnp.sum(grad_query.astype(jnp.float32), axis=0),
            jnp.sum(grad_value.astype(jnp.float32), axis=0),
        ]
    )
    grad_qkv_weight = jnp.einsum(
        "sd,jse->jde", whole_one, grad_qkv, preferred_element_type=jnp.float32
    )

    def qkv_back(offset, length):
        return jnp.einsum("jse,jde->sd", grad_qkv, w_qkv, preferred_element_type=jnp.float32)

    grad_normed_one = reduce_grads(qkv_back, row_count)
    grad_input = grad_residual + normalize_back(
        grad_normed_one, scaled_one, inverse_one, gain_rows[0]
    )
    grad_gain = jnp.stack(
        [
            jnp.sum(grad_normed_one * scaled_one, axis=0),
            jnp.sum(grad_normed_two * scaled_two, axis=0),
        ]
    )
    grad_bias = jnp.stack(
        [
            jnp.sum(grad_normed_one, axis=0),
            jnp.sum(grad_normed_two, axis=0),
            grad_proj_bias,
            grad_fc2_bias,
        ]
    )
    weight_part = (
        lax.psum_scatter(grad_qkv_weight, "dp", scatter_dimension=1, tiled=True),
        lax.psum_scatter(grad_proj, "dp", scatter_dimension=1, tiled=True),
        lax.psum_scatter(grad_fc1, "dp", scatter_dimension=0, tiled=True),
        lax.psum_scatter(grad_fc2, "dp", scatter_dimension=1, tiled=True),
        lax.psum_scatter(grad_qv, "dp", scatter_dimension=2, tiled=True),
        lax.psum_scatter(grad_fc1_bias.reshape(1, -1), "dp", scatter_dimension=1, tiled=True),
    )
    vector_part = (
        lax.psum_scatter(grad_gain, ("dp", "tensor"), scatter_dimension=1, tiled=True),
        lax.psum_scatter(grad_bias, ("dp", "tensor"), scatter_dimension=1, tiled=True),
    )
    return (grad_input, weight_part, vector_part)


def on_device(
    clip_rows,
    out_grad,
    clip_valid,
    gain_rows,
    bias_rows,
    qkv_weight,
    qv_bias,
    proj_weight,
    fc1_weight,
    fc1_bias,
    fc2_weight,
):
    clip_weight = clip_valid[0].astype(jnp.float32)
    upstream = out_grad.astype(jnp.float32) * clip_weight
    matrices, vectors = fetch(
        qkv_weight, proj_weight, fc1_weight, fc2_weight, qv_bias, fc1_bias, gain_rows, bias_rows
    )
    layer_out, stored = forward(clip_rows, matrices, vectors)
    matrices, vectors = fetch(
        qkv_weight, proj_weight, fc1_weight, fc2_weight, qv_bias, fc1_bias, gain_rows, bias_rows
    )
    unused_out, stored = forward(clip_rows, matrices, vectors)
    grad_input, weight_part, vector_part = backward(upstream, matrices, vectors, stored)
    return (
        (layer_out * clip_weight).astype(jnp.bfloat16),
        grad_input,
        vector_part[0],
        vector_part[1],
        weight_part[0],
        weight_part[4],
        weight_part[1],
        weight_part[2],
        weight_part[5],
        weight_part[3],
        vector_part[1][3],
    )


def solution(mesh):
    in_specs = (
        P(("dp", "tensor"), None),
        P(("dp", "tensor"), None),
        P("dp"),
        P(None, ("dp", "tensor")),
        P(None, ("dp", "tensor")),
        P(None, "dp", "tensor"),
        P(None, "tensor", "dp"),
        P("tensor", "dp"),
        P("dp", "tensor"),
        P("tensor", "dp"),
        P("tensor", "dp"),
    )
    out_specs = (
        P(("dp", "tensor"), None),
        P(("dp", "tensor"), None),
        P(None, ("dp", "tensor")),
        P(None, ("dp", "tensor")),
        P(None, "dp", "tensor"),
        P(None, "tensor", "dp"),
        P("tensor", "dp"),
        P("dp", "tensor"),
        P("tensor", "dp"),
        P("tensor", "dp"),
        P(("dp", "tensor")),
    )
    return jax.shard_map(
        on_device, mesh=mesh, in_specs=in_specs, out_specs=out_specs, check_vma=False
    )
```

profile of v0, /device:TPU:0, one launch (start us, length us, event | category | flops | bytes accessed | tf_op | source)
XLA Modules:
  0.0 1630.0 jit_solution(12553502785783311040)
XLA Ops:
  8.0 69.5 %all-gather = bf16[32,32,2]{1,2,0:T(2,128)(2,1)S(1)} all-gather(bf16[1,32,2]{1,2,0:T(2,128)(2,1)} %bitcast.144), channel_id=1, replica_groups=mesh['dp'=8,'tensor'=4] {'dp','tensor'}, dimensions={0}, use_global_device_ids=true | all-gather | bytes 4224 | tf_op jit(solution)/shard_map/all_gather | solution.py:51
  77.5 63.8 %all-gather.1 = bf16[32,32,4]{1,2,0:T(4,128)(2,1)S(1)} all-gather(bf16[1,32,4]{1,2,0:T(4,128)(2,1)} %bitcast.143), channel_id=1, replica_groups=mesh['dp'=8,'tensor'=4] {'dp','tensor'}, dimensions={0}, use_global_device_ids=true | all-gather | bytes 8448 | tf_op jit(solution)/shard_map/all_gather | solution.py:52
  146.4 8.1 all_gather.50
  154.6 11.0 all_gather.51
  165.6 43.3 %all-gather.10.cloned.1.call-done = bf16[1568,1024]{1,0:T(8,128)(2,1)} async-done(((bf16[392,1024]{1,0:T(8,128)(2,1)}), bf16[1568,1024]{1,0:T(8,128)(2,1)}) %all-gather.10.cloned.1.call-update) | async-done | bytes 3211280 | tf_op jit(solution)/shard_map/all_gather | solution.py:58
  208.9 5.1 convolution_bitcast_fusion.1
  221.3 16.1 fusion.48
  237.5 16.4 %fusion = f32[4,1568]{1,0:T(4,128)S(1)} fusion(f32[4,1568,1568]{1,2,0:T(8,128)} %get-tuple-element.82, f32[4,1568]{1,0:T(4,128)S(1)} %get-tuple-element.81), kind=kLoop, calls=%fused_computation.6 | loop fusion | flops 19662720 | bytes 39388160 | tf_op jit(solution)/shard_map/reduce_sum | solution.py:105
  253.8 17.4 %fusion.20 = bf16[4,64,1568]{2,1,0:T(8,128)(2,1)} fusion(f32[4,1568,1568]{1,2,0:T(8,128)} %get-tuple-element.82, f32[4,1568]{1,0:T(4,128)S(1)} %fusion, f32[4,1568]{1,0:T(4,128)S(1)} %get-tuple-element.81, f32[1568,4,64]{0,2,1:T(8,128)S(1)} %bitcast.106, f32[4,64]{1,0:T(4,128)S(1)} %copy.71), kind=kOutput, calls=%fused_computation.32 | convolution fusion | flops 1289523200 | bytes 41797632 | tf_op jit(solution)/shard_map/hqk,khd->qhd/dot_general | solution.py:109
  271.3 4.9 fusion.49
  277.2 110.7 %reduce-scatter.19.cloned.1.call-done = f32[392,1024]{1,0:T(8,128)} async-done(((f32[1568,1024]{1,0:T(8,128)}), f32[392,1024]{1,0:T(8,128)}) %reduce-scatter.19.cloned.1.call-update) | async-done | bytes 1605648 | tf_op jit(solution)/shard_map/reduce_scatter | solution.py:62
  393.6 8.7 all_gather.54
  402.4 15.7 all-gather.16.cloned.1.call-done
  418.1 66.6 %all-gather.14.cloned.1.call-done = bf16[1568,1024]{1,0:T(8,128)(2,1)} async-done(((bf16[392,1024]{1,0:T(8,128)(2,1)}), bf16[1568,1024]{1,0:T(8,128)(2,1)}) %all-gather.14.cloned.1.call-update) | async-done | bytes 3211280 | tf_op jit(solution)/shard_map/all_gather | solution.py:58
  484.7 8.5 multiply_convert_fusion.1
  493.2 20.1 %all-gather.18.cloned.1.call-done = bf16[1024,1024]{1,0:T(8,128)(2,1)} async-done(((bf16[1024,128]{1,0:T(8,128)(2,1)}), bf16[1024,1024]{1,0:T(8,128)(2,1)}) %all-gather.18.cloned.1.call-update) | async-done | bytes 2097168 | tf_op jit(solution)/shard_map/all_gather | solution.py:46
  513.3 66.8 %all-gather.20.cloned.1.call-done = bf16[1568,1024]{1,0:T(8,128)(2,1)} async-done(((bf16[392,1024]{1,0:T(8,128)(2,1)}), bf16[1568,1024]{1,0:T(8,128)(2,1)}) %all-gather.20.cloned.1.call-update) | async-done | bytes 3211280 | tf_op jit(solution)/shard_map/all_gather | solution.py:71
  580.0 9.5 convert_reduce_fusion
  591.3 5.7 fusion.51
  597.0 8.8 fusion.50
  605.9 102.8 %reduce-scatter.23.cloned.1.call-done = f32[392,1024]{1,0:T(8,128)} async-done(((f32[1568,1024]{1,0:T(8,128)}), f32[392,1024]{1,0:T(8,128)}) %reduce-scatter.23.cloned.1.call-update) | async-done | bytes 1605648 | tf_op jit(solution)/shard_map/reduce_scatter | solution.py:75
  708.6 2.1 multiply_reduce_fusion.1
  710.8 113.6 %reduce-scatter.21.cloned.1.call-done = f32[392,1024]{1,0:T(8,128)} async-done(((f32[1568,1024]{1,0:T(8,128)}), f32[392,1024]{1,0:T(8,128)}) %reduce-scatter.21.cloned.1.call-update) | async-done | bytes 1605648 | tf_op jit(solution)/shard_map/reduce_scatter | solution.py:62
  824.4 4.4 convert_reduce_fusion.5
  828.9 65.2 %all-gather.22.cloned.1.call-done = bf16[1568,1024]{1,0:T(8,128)(2,1)} async-done(((bf16[392,1024]{1,0:T(8,128)(2,1)}), bf16[1568,1024]{1,0:T(8,128)(2,1)}) %all-gather.22.cloned.1.call-update) | async-done | bytes 3211280 | tf_op jit(solution)/shard_map/all_gather | solution.py:71
  894.1 3.0 convolution_convert_fusion
  898.0 16.9 %convert_reduce_fusion.2 = (f32[4,64]{1,0:T(4,128)S(1)}, bf16[4,64,1568]{2,1,0:T(8,128)(2,1)}) fusion(bf16[1568,4,64]{0,2,1:T(8,128)(2,1)S(1)} %bitcast.104, f32[4,1568,1568]{1,2,0:T(8,128)} %get-tuple-element.82, f32[4,1568]{1,0:T(4,128)S(1)} %log_add_fusion), kind=kOutput, calls=%fused_computation.44 | convolution fusion | flops 1279688448 | bytes 40969728 | tf_op jit(solution)/shard_map/hqk,qhd->khd/dot_general | solution.py:213
  914.9 26.3 %multiply_reduce_fusion = (f32[4,1568]{1,0:T(4,128)S(1)}, f32[4,1568,1568]{1,2,0:T(8,128)}) fusion(f32[4,1568,1568]{1,2,0:T(8,128)} %get-tuple-element.82, f32[4,1568]{1,0:T(4,128)S(1)} %log_add_fusion, bf16[1568,4,64]{0,2,1:T(8,128)(2,1)S(1)} %bitcast.105, f32[1568,4,64]{0,2,1:T(8,128)S(1)} %bitcast.107, f32[4,64]{1,0:T(4,128)S(1)} %copy.71), kind=kOutput, calls=%fused_computation.1 | convolution fusion | flops 1289115520 | bytes 81135616 | tf_op jit(solution)/shard_map/qhd,khd->hqk/dot_general | solution.py:200
  941.2 33.6 %multiply_convert_fusion = bf16[4,1568,1568]{1,2,0:T(8,128)(2,1)} fusion(f32[4,1568,1568]{1,2,0:T(8,128)} %get-tuple-element.86, f32[4,1568,1568]{1,2,0:T(8,128)} %get-tuple-element.82, f32[4,1568]{1,0:T(4,128)S(1)} %get-tuple-element.85, f32[4,1568]{1,0:T(4,128)S(1)} %log_add_fusion), kind=kLoop, calls=%fused_computation | loop fusion | flops 39337984 | bytes 98395136 | tf_op jit(solution)/shard_map/convert_element_type | solution.py:204
  974.8 11.4 fusion.16
  986.2 10.4 convert_reduce_fusion.3
  999.9 7.3 convolution_bitcast_fusion
  1008.8 6.7 fusion.27
  1015.6 103.3 %reduce-scatter.25.cloned.1.call-done = f32[392,1024]{1,0:T(8,128)} async-done(((f32[1568,1024]{1,0:T(8,128)}), f32[392,1024]{1,0:T(8,128)}) %reduce-scatter.25.cloned.1.call-update) | async-done | bytes 1605648 | tf_op jit(solution)/shard_map/reduce_scatter | solution.py:75
  1119.0 2.2 fusion.36
  1123.4 8.8 fusion.53
  1132.6 8.9 fusion.54
  1142.7 4.0 fusion.52
  1148.0 8.6 reduce-scatter.39.cloned.1.call-done
  1158.0 12.2 all-reduce
  1170.9 35.7 %reduce-scatter.27.cloned.1.call-done = f32[3,128,256]{1,2,0:T(8,128)} async-done(((f32[3,1024,256]{1,2,0:T(8,128)}), f32[3,128,256]{1,2,0:T(8,128)}) %reduce-scatter.27.cloned.1.call-update) | async-done | bytes 393232 | tf_op jit(solution)/shard_map/reduce_scatter | solution.py:252
  1206.6 1.9 copy.83
  1208.5 3.1 fusion.35
  1211.7 131.5 %reduce-scatter.35.cloned.1.call-done = f32[32,2]{1,0:T(8,128)} async-done(((f32[1024,2]{1,0:T(8,128)}), f32[32,2]{1,0:T(8,128)}) %reduce-scatter.35.cloned.1.call-update) | async-done | bytes 272
  1344.6 131.6 %reduce-scatter.37.cloned.1.call-done = f32[32,4]{1,0:T(8,128)} async-done(((f32[1024,4]{1,0:T(8,128)}), f32[32,4]{1,0:T(8,128)}) %reduce-scatter.37.cloned.1.call-update) | async-done | bytes 528
  1477.5 50.1 %reduce-scatter.31.cloned.1.call-done = f32[128,1024]{1,0:T(8,128)} async-done(((f32[1024,1024]{1,0:T(8,128)}), f32[128,1024]{1,0:T(8,128)}) %reduce-scatter.31.cloned.1.call-update) | async-done | bytes 524304 | tf_op jit(solution)/shard_map/reduce_scatter | solution.py:254
  1527.6 55.5 %reduce-scatter.33.cloned.1.call-done = f32[1024,128]{1,0:T(8,128)} async-done(((f32[1024,1024]{1,0:T(8,128)}), f32[1024,128]{1,0:T(8,128)}) %reduce-scatter.33.cloned.1.call-update) | async-done | bytes 524304 | tf_op jit(solution)/shard_map/reduce_scatter | solution.py:255
  1583.1 39.6 %reduce-scatter.29.cloned.1.call-done = f32[256,128]{1,0:T(8,128)} async-done(((f32[256,1024]{1,0:T(8,128)}), f32[256,128]{1,0:T(8,128)}) %reduce-scatter.29.cloned.1.call-update) | async-done | bytes 131088 | tf_op jit(solution)/shard_map/reduce_scatter | solution.py:253
  (146 shorter events, 35.9 us)
Async XLA Ops:
  7.2 137.8 %copy-start.2 = (bf16[392,1024]{1,0:T(8,128)(2,1)S(1)}, bf16[392,1024]{1,0:T(8,128)(2,1)}, u32[]{:S(2)}) copy-start(bf16[392,1024]{1,0:T(8,128)(2,1)} %param.11) | copy-start | bytes 2408452
  7.2 158.4 %all-gather.12.cloned.1.call-start = ((), (), s32[]{:S(2)}) async-start(), calls=%async_computation.12 | async-start | bytes 1769472 | tf_op jit(solution)/shard_map/all_gather | solution.py:43
  7.9 201.0 %all-gather.10.cloned.1.call-start = ((), (), s32[]{:S(2)}) async-start(), calls=%async_computation.11 | async-start | bytes 4014080 | tf_op jit(solution)/shard_map/all_gather | solution.py:58
  141.3 4.9 copy-start.25
  141.4 13.2 copy-start.20
  142.8 71.2 %copy-start.21 = (f32[392]{0:T(512)}, f32[392]{0:T(512)S(1)}, u32[]{:S(2)}) copy-start(f32[392]{0:T(512)S(1)} %broadcast_multiply_fusion.5) | copy-start | bytes 4708
  144.3 69.7 %copy-start.23 = (f32[392]{0:T(512)}, f32[392]{0:T(512)S(1)}, u32[]{:S(2)}) copy-start(f32[392]{0:T(512)S(1)} %add_rsqrt_fusion.1) | copy-start | bytes 4708
  146.2 241.7 %reduce-scatter.19.cloned.1.call-start = ((), (), s32[]{:S(2)}) async-start(), calls=%async_computation.13 | async-start | bytes 8028160 | tf_op jit(solution)/shard_map/reduce_scatter | solution.py:62
  154.6 66.7 %copy-start.16 = (f32[4,64]{1,0:T(4,128)}, f32[4,64]{1,0:T(4,128)S(1)}, u32[]{:S(2)}) copy-start(f32[4,64]{1,0:T(4,128)S(1)} %copy.73) | copy-start | bytes 3076
  217.9 3.4 copy-start
  221.3 16.2 copy-start.3
  237.4 16.4 %copy-start.5 = (f32[1,1568,256]{1,2,0:T(8,128)S(1)}, f32[1,1568,256]{1,2,0:T(8,128)}, u32[]{:S(2)}) copy-start(f32[1,1568,256]{1,2,0:T(8,128)} %copy.69) | copy-start | bytes 4816900
  253.8 17.4 %copy-start.10 = (bf16[256,1024]{1,0:T(8,128)(2,1)S(1)}, bf16[256,1024]{1,0:T(8,128)(2,1)}, u32[]{:S(2)}) copy-start(bf16[256,1024]{1,0:T(8,128)(2,1)} %all_gather.51) | copy-start | bytes 1572868
  276.2 141.9 %all-gather.16.cloned.1.call-start = ((), (), s32[]{:S(2)}) async-start(), calls=%async_computation.15 | async-start | bytes 2359296 | tf_op jit(solution)/shard_map/all_gather | solution.py:45
  276.8 207.9 %all-gather.14.cloned.1.call-start = ((), (), s32[]{:S(2)}) async-start(), calls=%async_computation.14 | async-start | bytes 4014080 | tf_op jit(solution)/shard_map/all_gather | solution.py:58
  389.9 2.5 copy-start.9
  391.2 2.5 copy-start.27
  391.2 122.1 %all-gather.18.cloned.1.call-start = ((), (), s32[]{:S(2)}) async-start(), calls=%async_computation.16 | async-start | bytes 2359296 | tf_op jit(solution)/shard_map/all_gather | solution.py:46
  391.8 188.3 %all-gather.20.cloned.1.call-start = ((), (), s32[]{:S(2)}) async-start(), calls=%async_computation.18 | async-start | bytes 4014080 | tf_op jit(solution)/shard_map/all_gather | solution.py:71
  393.6 315.1 %reduce-scatter.23.cloned.1.call-start = ((), (), s32[]{:S(2)}) async-start(), calls=%async_computation.19 | async-start | bytes 8028160 | tf_op jit(solution)/shard_map/reduce_scatter | solution.py:75
  580.0 11.2 copy-start.28
  589.6 1.7 copy-start.30
  597.0 227.4 %reduce-scatter.21.cloned.1.call-start = ((), (), s32[]{:S(2)}) async-start(), calls=%async_computation.17 | async-start | bytes 8028160 | tf_op jit(solution)/shard_map/reduce_scatter | solution.py:62
  605.8 288.3 %all-gather.22.cloned.1.call-start = ((), (), s32[]{:S(2)}) async-start(), calls=%async_computation.20 | async-start | bytes 4014080 | tf_op jit(solution)/shard_map/all_gather | solution.py:71
  828.8 290.1 %reduce-scatter.25.cloned.1.call-start = ((), (), s32[]{:S(2)}) async-start(), calls=%async_computation.21 | async-start | bytes 8028160 | tf_op jit(solution)/shard_map/reduce_scatter | solution.py:75
  898.0 16.9 %copy-start.6 = (f32[1,1568,256]{1,2,0:T(8,128)S(1)}, f32[1,1568,256]{1,2,0:T(8,128)}, u32[]{:S(2)}) copy-start(f32[1,1568,256]{1,2,0:T(8,128)} %copy.69) | copy-start | bytes 4816900
  941.2 33.6 %copy-start.4 = (f32[1,1568,256]{1,2,0:T(8,128)S(1)}, f32[1,1568,256]{1,2,0:T(8,128)}, u32[]{:S(2)}) copy-start(f32[1,1568,256]{1,2,0:T(8,128)} %copy-done.3) | copy-start | bytes 4816900
  941.2 33.6 %copy-start.17 = (f32[4,64]{1,0:T(4,128)S(1)}, f32[4,64]{1,0:T(4,128)}, u32[]{:S(2)}) copy-start(f32[4,64]{1,0:T(4,128)} %copy-done.16) | copy-start | bytes 3076
  974.8 11.4 copy-start.1
  986.2 10.4 copy-start.8
  997.9 2.0 copy-start.12
  999.9 7.3 copy-start.14
  1007.2 1.2 copy-start.13
  1007.3 1.6 copy-start.15
  1007.3 149.3 %reduce-scatter.39.cloned.1.call-start = ((), (), s32[]{:S(2)}) async-start(), calls=%async_computation.28 | async-start | bytes 589824
  1008.4 198.2 %reduce-scatter.27.cloned.1.call-start = ((), (), s32[]{:S(2)}) async-start(), calls=%async_computation.22 | async-start | bytes 3538944 | tf_op jit(solution)/shard_map/reduce_scatter | solution.py:252
  1015.5 103.4 %copy-start.19 = (f32[1,1024]{1,0:T(1,128)S(1)}, f32[1,1024]{1,0:T(1,128)}, u32[]{:S(2)}) copy-start(f32[1,1024]{1,0:T(1,128)} %copy-done.18) | copy-start | bytes 12292
  1015.5 103.4 %copy-start.22 = (f32[392]{0:T(512)S(1)}, f32[392]{0:T(512)}, u32[]{:S(2)}) copy-start(f32[392]{0:T(512)} %copy-done.21) | copy-start | bytes 4708
  1015.5 103.4 %copy-start.24 = (f32[392]{0:T(512)S(1)}, f32[392]{0:T(512)}, u32[]{:S(2)}) copy-start(f32[392]{0:T(512)} %copy-done.23) | copy-start | bytes 4708
  1015.6 327.6 %reduce-scatter.35.cloned.1.call-start = ((), (), s32[]{:S(2)}) async-start(), calls=%async_computation.26 | async-start | bytes 540672
  1122.2 353.9 %reduce-scatter.37.cloned.1.call-start = ((), (), s32[]{:S(2)}) async-start(), calls=%async_computation.27 | async-start | bytes 540672
  1123.4 404.2 %reduce-scatter.31.cloned.1.call-start = ((), (), s32[]{:S(2)}) async-start(), calls=%async_computation.24 | async-start | bytes 4718592 | tf_op jit(solution)/shard_map/reduce_scatter | solution.py:254
  1132.3 450.8 %reduce-scatter.33.cloned.1.call-start = ((), (), s32[]{:S(2)}) async-start(), calls=%async_computation.25 | async-start | bytes 4718592 | tf_op jit(solution)/shard_map/reduce_scatter | solution.py:255
  1141.5 1.2 copy-start.11
  1141.5 5.2 copy-start.29
  1141.5 481.2 %reduce-scatter.29.cloned.1.call-start = ((), (), s32[]{:S(2)}) async-start(), calls=%async_computation.23 | async-start | bytes 1179648 | tf_op jit(solution)/shard_map/reduce_scatter | solution.py:253
  1146.7 61.8 %copy-start.7 = (f32[392,1024]{1,0:T(8,128)S(1)}, f32[392,1024]{1,0:T(8,128)}, u32[]{:S(2)}) copy-start(f32[392,1024]{1,0:T(8,128)} %reduce-scatter.25.cloned.1.call-done) | copy-start | bytes 4816900
  1476.9 145.8 %copy-start.26 = (f32[4,32]{1,0:T(4,128)}, f32[4,32]{1,0:T(4,128)S(1)}, u32[]{:S(2)}) copy-start(f32[4,32]{1,0:T(4,128)S(1)} %copy.91) | copy-start | bytes 1540
  (1 other events, 0.6 us)
Sparse Core Ops, SparseCore 0:
  9.9 28.3 all-gather.11
  146.3 62.5 all-gather.9
  276.3 111.5 reduce-scatter.18
  389.6 28.3 all-gather.15
  420.1 64.5 all-gather.13
  486.4 26.8 all-gather.17
  515.4 64.5 all-gather.19
  597.1 111.5 reduce-scatter.22
  711.0 113.3 reduce-scatter.20
  829.0 65.0 all-gather.21
  1007.4 111.5 reduce-scatter.24
  1121.9 34.6 reduce-scatter.38
  1160.3 46.2 reduce-scatter.26
  1208.7 134.4 reduce-scatter.34
  1345.4 130.7 reduce-scatter.36
  1479.9 47.6 reduce-scatter.30
  1531.7 51.3 reduce-scatter.32
  1586.7 35.9 reduce-scatter.28
where the time goes:
time: 1640 us; the launch traced here: 1630 us
  waiting for transfers between devices  1160 us (71%)
  matrix products  180 us (11%)
  blocking collectives  173 us (11%)
  other arithmetic  70.3 us (4%)
  local copies, waits for them, and re-layouts  26 us (2%)
  between operations  16.5 us (1%)
    unnamed x21, waiting for transfers between devices  274 us
    reduce_scatter x2, waiting for transfers between devices, reduce_rows(): lax.psum_scatter(term_fn(jnp.int32(0), lax.axis_size('tensor') * row_coun...  224 us
    reduce_scatter x2, waiting for transfers between devices, reduce_grads(): lax.psum_scatter(term_fn(jnp.int32(0), lax.axis_size('tensor') * row_coun...  206 us
    all_gather x2, waiting for transfers between devices, spread_grads(): return lax.all_gather(local_rows, 'tensor', axis=0, tiled=True)  132 us
    all_gather x2, waiting for transfers between devices, spread_rows(): return lax.all_gather(local_rows, 'tensor', axis=0, tiled=True)  110 us
    all_gather x1, blocking collectives, fetch(): lax.all_gather(gain_rows, ('dp', 'tensor'), axis=1, tiled=True)  69.5 us
    all_gather x1, blocking collectives, fetch(): lax.all_gather(bias_rows, ('dp', 'tensor'), axis=1, tiled=True)  63.8 us
    reduce_scatter x1, waiting for transfers between devices, backward(): lax.psum_scatter(grad_fc2, 'dp', scatter_dimension=1, tiled=True)  55.5 us
  transfers between devices with their start and end apart: 18, of which 17 were waited for; matrix products, arithmetic and copies ran while one was open for 4% of the time, Pallas kernels for 0%

commit v1 on v0

--- a/solution.py
+++ b/solution.py
@@ -8,6 +8,25 @@
 norm_eps = 1e-06
 root_half = 0.7071067811865476
 inv_root_tau = 0.3989422804014327
+
+
+def ring_gather(shard, axis, dim):
+    size, mine, rows = (lax.axis_size(axis), lax.axis_index(axis), shard.shape[dim])
+    forward = [(i, (i + 1) % size) for i in range(size)]
+    backward = [(i, (i - 1) % size) for i in range(size)]
+    out = jnp.zeros((*shard.shape[:dim], size * rows, *shard.shape[dim + 1 :]), shard.dtype)
+    out = lax.dynamic_update_slice_in_dim(out, shard, mine * rows, axis=dim)
+    from_left = from_right = shard
+    half = size // 2
+    for step in range(1, half + 1):
+        from_left = lax.ppermute(from_left, axis, forward)
+        out = lax.dynamic_update_slice_in_dim(out, from_left, (mine - step) % size * rows, axis=dim)
+        if step < size - half:
+            from_right = lax.ppermute(from_right, axis, backward)
+            out = lax.dynamic_update_slice_in_dim(
+                out, from_right, (mine + step) % size * rows, axis=dim
+            )
+    return out
 
 
 def normalize(values, gain_row, shift_row):
@@ -55,7 +74,7 @@
 
 
 def spread_rows(local_rows):
-    return lax.all_gather(local_rows, "tensor", axis=0, tiled=True)
+    return ring_gather(local_rows, "tensor", 0)
 
 
 def reduce_rows(term_fn, row_count):

time: 1640 us -> 1560 us (0.951)
  waiting for transfers between devices: 1160 us -> 1050 us
  starting transfers between devices: 1.33 us -> 33.2 us
    all_gather x2 -> x0, waiting for transfers between devices: 110 us -> none  [spread_rows(): return lax.all_gather(local_rows, 'tensor', axis=0, tiled=True)]
    ppermute x0 -> x6, waiting for transfers between devices: none -> 45.6 us  [the longest x4 45.6 us: ring_gather(): from_left = lax.ppermute(from_left, axis, forward)]
    ppermute x0 -> x6, starting transfers between devices: none -> 31.7 us  [the longest x4 27.8 us: ring_gather(): from_left = lax.ppermute(from_left, axis, forward)]
    all_gather x1, waiting for transfers between devices: 20.1 us -> 0.01 us  [fetch(): lax.all_gather(fc2_weight, 'dp', axis=1, tiled=True)]
    unnamed x21 -> x19, waiting for transfers between devices: 274 us -> 273 us
  transfers between devices with their start and end apart: 18 -> 22, of which waited for: 17 -> 16; matrix products, arithmetic and copies ran while one was open for 4% -> 5% of each run, Pallas kernels for 0% -> 0%
where the time goes in v1:
time: 1560 us
  waiting for transfers between devices  1050 us (67%)
  matrix products  180 us (12%)
  blocking collectives  173 us (11%)
  other arithmetic  70.3 us (5%)
  local copies, waits for them, and re-layouts  36.3 us (2%)
  starting transfers between devices  33.2 us (2%)
  between operations  15.9 us (1%)
    unnamed x19, waiting for transfers between devices  273 us
    reduce_scatter x2, waiting for transfers between devices, reduce_rows(): lax.psum_scatter(term_fn(jnp.int32(0), lax.axis_size('tensor') * row_coun...  223 us
    reduce_scatter x2, waiting for transfers between devices, reduce_grads(): lax.psum_scatter(term_fn(jnp.int32(0), lax.axis_size('tensor') * row_coun...  206 us
    all_gather x2, waiting for transfers between devices, spread_grads(): return lax.all_gather(local_rows, 'tensor', axis=0, tiled=True)  121 us
    all_gather x1, blocking collectives, fetch(): lax.all_gather(gain_rows, ('dp', 'tensor'), axis=1, tiled=True)  69.6 us
    all_gather x1, blocking collectives, fetch(): lax.all_gather(bias_rows, ('dp', 'tensor'), axis=1, tiled=True)  63.7 us
    reduce_scatter x1, waiting for transfers between devices, backward(): lax.psum_scatter(grad_fc2, 'dp', scatter_dimension=1, tiled=True)  55.5 us
    reduce_scatter x1, waiting for transfers between devices, backward(): lax.psum_scatter(grad_fc1, 'dp', scatter_dimension=0, tiled=True)  50.1 us
  transfers between devices with their start and end apart: 22, of which 16 were waited for; matrix products, arithmetic and copies ran while one was open for 5% of the time, Pallas kernels for 0%

profile of v1, /device:TPU:0, one launch (start us, length us, event | category | flops | bytes accessed | tf_op | source)
XLA Modules:
  0.0 1559.0 jit_solution(508841865736207487)
XLA Ops:
  9.3 69.6 %all-gather = bf16[32,32,2]{1,2,0:T(2,128)(2,1)S(1)} all-gather(bf16[1,32,2]{1,2,0:T(2,128)(2,1)} %bitcast.144), channel_id=1, replica_groups=mesh['dp'=8,'tensor'=4] {'dp','tensor'}, dimensions={0}, use_global_device_ids=true | all-gather | bytes 4224 | tf_op jit(solution)/shard_map/all_gather | solution.py:70
  78.9 63.7 %all-gather.1 = bf16[32,32,4]{1,2,0:T(4,128)(2,1)S(1)} all-gather(bf16[1,32,4]{1,2,0:T(4,128)(2,1)} %bitcast.143), channel_id=1, replica_groups=mesh['dp'=8,'tensor'=4] {'dp','tensor'}, dimensions={0}, use_global_device_ids=true | all-gather | bytes 8448 | tf_op jit(solution)/shard_map/all_gather | solution.py:71
  147.8 2.3 collective-permute-start
  151.7 18.8 %collective-permute-done = bf16[392,1024]{1,0:T(8,128)(2,1)S(1)} collective-permute-done((bf16[392,1024]{1,0:T(8,128)(2,1)S(1)}, bf16[392,1024]{1,0:T(8,128)(2,1)S(1)}, u32[]{:S(2)}, u32[]{:S(2)}) %collective-permute-start) | collective-permute-done | bytes 802848 | tf_op jit(solution)/shard_map/ppermute | solution.py:22
  170.5 9.4 collective-permute-start.2
  180.0 8.1 all_gather.41
  188.2 11.2 all_gather.42
  203.4 5.1 convolution_bitcast_fusion.1
  215.8 16.1 %fusion.49 = (f32[4,1568]{1,0:T(4,128)S(1)}, f32[4,1568,1568]{1,2,0:T(8,128)}) fusion(bf16[1568,4,64]{0,2,1:T(8,128)(2,1)S(1)} %bitcast.99, f32[1568,4,64]{0,2,1:T(8,128)S(1)} %bitcast.102, f32[4,64]{1,0:T(4,128)S(1)} %copy.73), kind=kOutput, calls=%fused_computation.102 | convolution fusion | flops 1279281024 | bytes 41772544 | tf_op jit(solution)/shard_map/qhd,khd->hqk/dot_general | solution.py:119
  231.9 16.4 %fusion = f32[4,1568]{1,0:T(4,128)S(1)} fusion(f32[4,1568,1568]{1,2,0:T(8,128)} %get-tuple-element.86, f32[4,1568]{1,0:T(4,128)S(1)} %get-tuple-element.85), kind=kLoop, calls=%fused_computation.6 | loop fusion | flops 19662720 | bytes 39388160 | tf_op jit(solution)/shard_map/reduce_sum | solution.py:124
  248.3 17.4 %fusion.20 = bf16[4,64,1568]{2,1,0:T(8,128)(2,1)} fusion(f32[4,1568,1568]{1,2,0:T(8,128)} %get-tuple-element.86, f32[4,1568]{1,0:T(4,128)S(1)} %fusion, f32[4,1568]{1,0:T(4,128)S(1)} %get-tuple-element.85, f32[1568,4,64]{0,2,1:T(8,128)S(1)} %bitcast.106, f32[4,64]{1,0:T(4,128)S(1)} %copy.71), kind=kOutput, calls=%fused_computation.32 | convolution fusion | flops 1289523200 | bytes 41797632 | tf_op jit(solution)/shard_map/hqk,khd->qhd/dot_general | solution.py:128
  265.7 4.9 fusion.50
  273.8 109.5 %reduce-scatter.19.cloned.1.call-done = f32[392,1024]{1,0:T(8,128)} async-done(((f32[1568,1024]{1,0:T(8,128)}), f32[392,1024]{1,0:T(8,128)}) %reduce-scatter.19.cloned.1.call-update) | async-done | bytes 1605648 | tf_op jit(solution)/shard_map/reduce_scatter | solution.py:81
  390.3 2.3 collective-permute-start.4
  392.6 18.8 %collective-permute-done.3 = bf16[392,1024]{1,0:T(8,128)(2,1)S(1)} collective-permute-done((bf16[392,1024]{1,0:T(8,128)(2,1)S(1)}, bf16[392,1024]{1,0:T(8,128)(2,1)S(1)}, u32[]{:S(2)}, u32[]{:S(2)}) %collective-permute-start.3) | collective-permute-done | bytes 802848 | tf_op jit(solution)/shard_map/ppermute | solution.py:22
  411.4 14.6 collective-permute-start.5
  426.0 8.7 all_gather.44
  436.7 8.0 collective-permute-done.5
  445.6 8.5 multiply_convert_fusion.1
  454.2 56.1 %all-gather.14.cloned.1.call-done = bf16[1568,1024]{1,0:T(8,128)(2,1)} async-done(((bf16[392,1024]{1,0:T(8,128)(2,1)}), bf16[1568,1024]{1,0:T(8,128)(2,1)}) %all-gather.14.cloned.1.call-update) | async-done | bytes 3211280 | tf_op jit(solution)/shard_map/all_gather | solution.py:90
  510.3 9.5 convert_reduce_fusion
  521.5 5.7 fusion.52
  527.3 8.8 fusion.51
  536.3 102.6 %reduce-scatter.23.cloned.1.call-done = f32[392,1024]{1,0:T(8,128)} async-done(((f32[1568,1024]{1,0:T(8,128)}), f32[392,1024]{1,0:T(8,128)}) %reduce-scatter.23.cloned.1.call-update) | async-done | bytes 1605648 | tf_op jit(solution)/shard_map/reduce_scatter | solution.py:94
  641.0 113.6 %reduce-scatter.21.cloned.1.call-done = f32[392,1024]{1,0:T(8,128)} async-done(((f32[1568,1024]{1,0:T(8,128)}), f32[392,1024]{1,0:T(8,128)}) %reduce-scatter.21.cloned.1.call-update) | async-done | bytes 1605648 | tf_op jit(solution)/shard_map/reduce_scatter | solution.py:81
  754.6 4.4 convert_reduce_fusion.5
  759.1 65.2 %all-gather.16.cloned.1.call-done = bf16[1568,1024]{1,0:T(8,128)(2,1)} async-done(((bf16[392,1024]{1,0:T(8,128)(2,1)}), bf16[1568,1024]{1,0:T(8,128)(2,1)}) %all-gather.16.cloned.1.call-update) | async-done | bytes 3211280 | tf_op jit(solution)/shard_map/all_gather | solution.py:90
  824.3 3.0 convolution_convert_fusion
  828.1 16.9 %convert_reduce_fusion.2 = (f32[4,64]{1,0:T(4,128)S(1)}, bf16[4,64,1568]{2,1,0:T(8,128)(2,1)}) fusion(bf16[1568,4,64]{0,2,1:T(8,128)(2,1)S(1)} %bitcast.104, f32[4,1568,1568]{1,2,0:T(8,128)} %get-tuple-element.86, f32[4,1568]{1,0:T(4,128)S(1)} %log_add_fusion), kind=kOutput, calls=%fused_computation.44 | convolution fusion | flops 1279688448 | bytes 40969728 | tf_op jit(solution)/shard_map/hqk,qhd->khd/dot_general | solution.py:232
  845.0 26.4 %multiply_reduce_fusion = (f32[4,1568]{1,0:T(4,128)S(1)}, f32[4,1568,1568]{1,2,0:T(8,128)}) fusion(f32[4,1568,1568]{1,2,0:T(8,128)} %get-tuple-element.86, f32[4,1568]{1,0:T(4,128)S(1)} %log_add_fusion, bf16[1568,4,64]{0,2,1:T(8,128)(2,1)S(1)} %bitcast.105, f32[1568,4,64]{0,2,1:T(8,128)S(1)} %bitcast.107, f32[4,64]{1,0:T(4,128)S(1)} %copy.71), kind=kOutput, calls=%fused_computation.1 | convolution fusion | flops 1289115520 | bytes 81135616 | tf_op jit(solution)/shard_map/qhd,khd->hqk/dot_general | solution.py:219
  871.3 33.5 %multiply_convert_fusion = bf16[4,1568,1568]{1,2,0:T(8,128)(2,1)} fusion(f32[4,1568,1568]{1,2,0:T(8,128)} %get-tuple-element.90, f32[4,1568,1568]{1,2,0:T(8,128)} %get-tuple-element.86, f32[4,1568]{1,0:T(4,128)S(1)} %get-tuple-element.89, f32[4,1568]{1,0:T(4,128)S(1)} %log_add_fusion), kind=kLoop, calls=%fused_computation | loop fusion | flops 39337984 | bytes 98395136 | tf_op jit(solution)/shard_map/convert_element_type | solution.py:223
  904.9 11.4 fusion.16
  916.3 10.4 convert_reduce_fusion.3
  929.9 7.3 convolution_bitcast_fusion
  938.9 6.7 fusion.27
  945.7 103.3 %reduce-scatter.25.cloned.1.call-done = f32[392,1024]{1,0:T(8,128)} async-done(((f32[1568,1024]{1,0:T(8,128)}), f32[392,1024]{1,0:T(8,128)}) %reduce-scatter.25.cloned.1.call-update) | async-done | bytes 1605648 | tf_op jit(solution)/shard_map/reduce_scatter | solution.py:94
  1053.4 8.8 fusion.54
  1062.6 8.9 fusion.55
  1072.8 4.0 fusion.53
  1078.0 8.6 reduce-scatter.39.cloned.1.call-done
  1088.1 12.2 all-reduce
  1100.9 35.8 %reduce-scatter.27.cloned.1.call-done = f32[3,128,256]{1,2,0:T(8,128)} async-done(((f32[3,1024,256]{1,2,0:T(8,128)}), f32[3,128,256]{1,2,0:T(8,128)}) %reduce-scatter.27.cloned.1.call-update) | async-done | bytes 393232 | tf_op jit(solution)/shard_map/reduce_scatter | solution.py:271
  1138.6 3.1 fusion.35
  1141.7 131.2 %reduce-scatter.35.cloned.1.call-done = f32[32,2]{1,0:T(8,128)} async-done(((f32[1024,2]{1,0:T(8,128)}), f32[32,2]{1,0:T(8,128)}) %reduce-scatter.35.cloned.1.call-update) | async-done | bytes 272
  1274.3 131.3 %reduce-scatter.37.cloned.1.call-done = f32[32,4]{1,0:T(8,128)} async-done(((f32[1024,4]{1,0:T(8,128)}), f32[32,4]{1,0:T(8,128)}) %reduce-scatter.37.cloned.1.call-update) | async-done | bytes 528
  1406.9 50.1 %reduce-scatter.31.cloned.1.call-done = f32[128,1024]{1,0:T(8,128)} async-done(((f32[1024,1024]{1,0:T(8,128)}), f32[128,1024]{1,0:T(8,128)}) %reduce-scatter.31.cloned.1.call-update) | async-done | bytes 524304 | tf_op jit(solution)/shard_map/reduce_scatter | solution.py:273
  1457.0 55.5 %reduce-scatter.33.cloned.1.call-done = f32[1024,128]{1,0:T(8,128)} async-done(((f32[1024,1024]{1,0:T(8,128)}), f32[1024,128]{1,0:T(8,128)}) %reduce-scatter.33.cloned.1.call-update) | async-done | bytes 524304 | tf_op jit(solution)/shard_map/reduce_scatter | solution.py:274
  1512.5 39.6 %reduce-scatter.29.cloned.1.call-done = f32[256,128]{1,0:T(8,128)} async-done(((f32[256,1024]{1,0:T(8,128)}), f32[256,128]{1,0:T(8,128)}) %reduce-scatter.29.cloned.1.call-update) | async-done | bytes 131088 | tf_op jit(solution)/shard_map/reduce_scatter | solution.py:272
  (160 shorter events, 55.5 us)
Async XLA Ops:
  7.2 196.2 %all-gather.8.cloned.1.call-start = ((), (), s32[]{:S(2)}) async-start(), calls=%async_computation.11 | async-start | bytes 1769472 | tf_op jit(solution)/shard_map/all_gather | solution.py:62
  7.9 375.5 %reduce-scatter.19.cloned.1.call-start = ((), (), s32[]{:S(2)}) async-start(), calls=%async_computation.12 | async-start | bytes 8028160 | tf_op jit(solution)/shard_map/reduce_scatter | solution.py:81
  9.3 137.2 %copy-start.2 = (bf16[392,1024]{1,0:T(8,128)(2,1)S(1)}, bf16[392,1024]{1,0:T(8,128)(2,1)}, u32[]{:S(2)}) copy-start(bf16[392,1024]{1,0:T(8,128)(2,1)} %param.11) | copy-start | bytes 2408452
  9.3 138.5 %copy-start.21 = (f32[392]{0:T(512)}, f32[392]{0:T(512)S(1)}, u32[]{:S(2)}) copy-start(f32[392]{0:T(512)S(1)} %broadcast_multiply_fusion.5) | copy-start | bytes 4708
  144.4 3.4 copy-start.23
  144.4 3.4 copy-start.18
  144.4 35.4 %copy-start.25 = (bf16[2,4,8]{2,1,0:T(4,128)(2,1)S(1)}, bf16[2,4,8]{2,1,0:T(4,128)(2,1)}, u32[]{:S(2)}) copy-start(bf16[2,4,8]{2,1,0:T(4,128)(2,1)} %param.17) | copy-start | bytes 388
  144.4 43.8 %copy-start.20 = (bf16[256,128]{1,0:T(8,128)(2,1)S(1)}, bf16[256,128]{1,0:T(8,128)(2,1)}, u32[]{:S(2)}) copy-start(bf16[256,128]{1,0:T(8,128)(2,1)} %param.18) | copy-start | bytes 196612
  147.8 22.7 %collective-permute-start = (bf16[392,1024]{1,0:T(8,128)(2,1)S(1)}, bf16[392,1024]{1,0:T(8,128)(2,1)S(1)}, u32[]{:S(2)}, u32[]{:S(2)}) collective-permute-start(bf16[392,1024]{1,0:T(8,128)(2,1)S(1)} %get-tuple-element.73), channel_id=1, source_target_pairs={{0,1},{1,2},{2,3},{3,0},{4,5},{5,6},{6,7},{7,4},{8,9},{9,10},{10,1... | collective-permute-start | bytes 2408456 | tf_op jit(solution)/shard_map/ppermute | solution.py:22
  150.0 50.3 %collective-permute-start.1 = (bf16[392,1024]{1,0:T(8,128)(2,1)S(1)}, bf16[392,1024]{1,0:T(8,128)(2,1)S(1)}, u32[]{:S(2)}, u32[]{:S(2)}) collective-permute-start(bf16[392,1024]{1,0:T(8,128)(2,1)S(1)} %get-tuple-element.73), channel_id=1, source_target_pairs={{0,3},{1,0},{2,1},{3,2},{4,7},{5,4},{6,5},{7,6},{8,11},{9,8},{10,9... | collective-permute-start | bytes 2408456 | tf_op jit(solution)/shard_map/ppermute | solution.py:25
  170.5 30.8 %collective-permute-start.2 = (bf16[392,1024]{1,0:T(8,128)(2,1)S(1)}, bf16[392,1024]{1,0:T(8,128)(2,1)}, u32[]{:S(2)}, u32[]{:S(2)}) collective-permute-start(bf16[392,1024]{1,0:T(8,128)(2,1)S(1)} %collective-permute-done), channel_id=1, source_target_pairs={{0,1},{1,2},{2,3},{3,0},{4,5},{5,6},{6,7},{7,4},{8,9},{9,10},{10,1... | collective-permute-start | bytes 2408456 | tf_op jit(solution)/shard_map/ppermute | solution.py:22
  188.2 27.5 %copy-start.16 = (f32[4,64]{1,0:T(4,128)}, f32[4,64]{1,0:T(4,128)S(1)}, u32[]{:S(2)}) copy-start(f32[4,64]{1,0:T(4,128)S(1)} %copy.73) | copy-start | bytes 3076
  212.3 3.4 copy-start
  215.7 16.2 %copy-start.3 = (f32[1,1568,256]{1,2,0:T(8,128)}, f32[1,1568,256]{1,2,0:T(8,128)S(1)}, u32[]{:S(2)}) copy-start(f32[1,1568,256]{1,2,0:T(8,128)S(1)} %copy.72) | copy-start | bytes 4816900
  231.9 16.4 %copy-start.5 = (f32[1,1568,256]{1,2,0:T(8,128)S(1)}, f32[1,1568,256]{1,2,0:T(8,128)}, u32[]{:S(2)}) copy-start(f32[1,1568,256]{1,2,0:T(8,128)} %copy.69) | copy-start | bytes 4816900
  248.3 17.4 %copy-start.10 = (bf16[256,1024]{1,0:T(8,128)(2,1)S(1)}, bf16[256,1024]{1,0:T(8,128)(2,1)}, u32[]{:S(2)}) copy-start(bf16[256,1024]{1,0:T(8,128)(2,1)} %all_gather.42) | copy-start | bytes 1572868
  270.6 2.0 copy-start.9
  270.7 174.9 %all-gather.10.cloned.1.call-start = ((), (), s32[]{:S(2)}) async-start(), calls=%async_computation.13 | async-start | bytes 2359296 | tf_op jit(solution)/shard_map/all_gather | solution.py:64
  271.4 182.8 %all-gather.12.cloned.1.call-start = ((), (), s32[]{:S(2)}) async-start(), calls=%async_computation.14 | async-start | bytes 2359296 | tf_op jit(solution)/shard_map/all_gather | solution.py:65
  272.0 238.3 %all-gather.14.cloned.1.call-start = ((), (), s32[]{:S(2)}) async-start(), calls=%async_computation.16 | async-start | bytes 4014080 | tf_op jit(solution)/shard_map/all_gather | solution.py:90
  273.8 365.1 %reduce-scatter.23.cloned.1.call-start = ((), (), s32[]{:S(2)}) async-start(), calls=%async_computation.17 | async-start | bytes 8028160 | tf_op jit(solution)/shard_map/reduce_scatter | solution.py:94
  387.5 38.5 %copy-start.27 = (bf16[1,128]{1,0:T(2,128)(2,1)S(1)}, bf16[1,128]{1,0:T(2,128)(2,1)}, u32[]{:S(2)}) copy-start(bf16[1,128]{1,0:T(2,128)(2,1)} %param.20) | copy-start | bytes 772
  388.7 22.6 %collective-permute-start.3 = (bf16[392,1024]{1,0:T(8,128)(2,1)S(1)}, bf16[392,1024]{1,0:T(8,128)(2,1)S(1)}, u32[]{:S(2)}, u32[]{:S(2)}) collective-permute-start(bf16[392,1024]{1,0:T(8,128)(2,1)S(1)} %get-tuple-element.69), channel_id=1, source_target_pairs={{0,1},{1,2},{2,3},{3,0},{4,5},{5,6},{6,7},{7,4},{8,9},{9,10},{10,1... | collective-permute-start | bytes 2408456 | tf_op jit(solution)/shard_map/ppermute | solution.py:22
  390.3 45.4 %collective-permute-start.4 = (bf16[392,1024]{1,0:T(8,128)(2,1)S(1)}, bf16[392,1024]{1,0:T(8,128)(2,1)S(1)}, u32[]{:S(2)}, u32[]{:S(2)}) collective-permute-start(bf16[392,1024]{1,0:T(8,128)(2,1)S(1)} %get-tuple-element.69), channel_id=1, source_target_pairs={{0,3},{1,0},{2,1},{3,2},{4,7},{5,4},{6,5},{7,6},{8,11},{9,8},{10,9... | collective-permute-start | bytes 2408456 | tf_op jit(solution)/shard_map/ppermute | solution.py:25
  411.4 33.3 %collective-permute-start.5 = (bf16[392,1024]{1,0:T(8,128)(2,1)S(1)}, bf16[392,1024]{1,0:T(8,128)(2,1)S(1)}, u32[]{:S(2)}, u32[]{:S(2)}) collective-permute-start(bf16[392,1024]{1,0:T(8,128)(2,1)S(1)} %collective-permute-done.3), channel_id=1, source_target_pairs={{0,1},{1,2},{2,3},{3,0},{4,5},{5,6},{6,7},{7,4},{8,9},{9,10},{10,1... | collective-permute-start | bytes 2408456 | tf_op jit(solution)/shard_map/ppermute | solution.py:22
  510.3 11.2 copy-start.28
  527.2 227.4 %reduce-scatter.21.cloned.1.call-start = ((), (), s32[]{:S(2)}) async-start(), calls=%async_computation.15 | async-start | bytes 8028160 | tf_op jit(solution)/shard_map/reduce_scatter | solution.py:81
  536.1 288.3 %all-gather.16.cloned.1.call-start = ((), (), s32[]{:S(2)}) async-start(), calls=%async_computation.18 | async-start | bytes 4014080 | tf_op jit(solution)/shard_map/all_gather | solution.py:90
  759.1 289.9 %reduce-scatter.25.cloned.1.call-start = ((), (), s32[]{:S(2)}) async-start(), calls=%async_computation.19 | async-start | bytes 8028160 | tf_op jit(solution)/shard_map/reduce_scatter | solution.py:94
  828.0 16.9 %copy-start.6 = (f32[1,1568,256]{1,2,0:T(8,128)S(1)}, f32[1,1568,256]{1,2,0:T(8,128)}, u32[]{:S(2)}) copy-start(f32[1,1568,256]{1,2,0:T(8,128)} %copy.69) | copy-start | bytes 4816900
  871.3 33.5 %copy-start.4 = (f32[1,1568,256]{1,2,0:T(8,128)S(1)}, f32[1,1568,256]{1,2,0:T(8,128)}, u32[]{:S(2)}) copy-start(f32[1,1568,256]{1,2,0:T(8,128)} %copy-done.3) | copy-start | bytes 4816900
  871.3 33.5 %copy-start.17 = (f32[4,64]{1,0:T(4,128)S(1)}, f32[4,64]{1,0:T(4,128)}, u32[]{:S(2)}) copy-start(f32[4,64]{1,0:T(4,128)} %copy-done.16) | copy-start | bytes 3076
  904.9 11.4 copy-start.1
  916.3 10.4 copy-start.8
  929.9 7.4 copy-start.14
  937.3 149.3 %reduce-scatter.39.cloned.1.call-start = ((), (), s32[]{:S(2)}) async-start(), calls=%async_computation.26 | async-start | bytes 589824
  938.4 198.2 %reduce-scatter.27.cloned.1.call-start = ((), (), s32[]{:S(2)}) async-start(), calls=%async_computation.20 | async-start | bytes 3538944 | tf_op jit(solution)/shard_map/reduce_scatter | solution.py:271
  945.6 103.4 %copy-start.19 = (f32[1,1024]{1,0:T(1,128)S(1)}, f32[1,1024]{1,0:T(1,128)}, u32[]{:S(2)}) copy-start(f32[1,1024]{1,0:T(1,128)} %copy-done.18) | copy-start | bytes 12292
  945.6 103.4 %copy-start.22 = (f32[392]{0:T(512)S(1)}, f32[392]{0:T(512)}, u32[]{:S(2)}) copy-start(f32[392]{0:T(512)} %copy-done.21) | copy-start | bytes 4708
  945.6 103.4 %copy-start.24 = (f32[392]{0:T(512)S(1)}, f32[392]{0:T(512)}, u32[]{:S(2)}) copy-start(f32[392]{0:T(512)} %copy-done.23) | copy-start | bytes 4708
  945.6 327.3 %reduce-scatter.35.cloned.1.call-start = ((), (), s32[]{:S(2)}) async-start(), calls=%async_computation.24 | async-start | bytes 540672
  1052.3 353.3 %reduce-scatter.37.cloned.1.call-start = ((), (), s32[]{:S(2)}) async-start(), calls=%async_computation.25 | async-start | bytes 540672
  1053.4 403.6 %reduce-scatter.31.cloned.1.call-start = ((), (), s32[]{:S(2)}) async-start(), calls=%async_computation.22 | async-start | bytes 4718592 | tf_op jit(solution)/shard_map/reduce_scatter | solution.py:273
  1062.3 450.2 %reduce-scatter.33.cloned.1.call-start = ((), (), s32[]{:S(2)}) async-start(), calls=%async_computation.23 | async-start | bytes 4718592 | tf_op jit(solution)/shard_map/reduce_scatter | solution.py:274
  1071.6 5.2 copy-start.29
  1071.6 480.6 %reduce-scatter.29.cloned.1.call-start = ((), (), s32[]{:S(2)}) async-start(), calls=%async_computation.21 | async-start | bytes 1179648 | tf_op jit(solution)/shard_map/reduce_scatter | solution.py:272
  1076.8 61.8 %copy-start.7 = (f32[392,1024]{1,0:T(8,128)S(1)}, f32[392,1024]{1,0:T(8,128)}, u32[]{:S(2)}) copy-start(f32[392,1024]{1,0:T(8,128)} %reduce-scatter.25.cloned.1.call-done) | copy-start | bytes 4816900
  1406.4 145.8 %copy-start.26 = (f32[4,32]{1,0:T(4,128)}, f32[4,32]{1,0:T(4,128)S(1)}, u32[]{:S(2)}) copy-start(f32[4,32]{1,0:T(4,128)S(1)} %copy.91) | copy-start | bytes 1540
  (5 other events, 7.7 us)
Sparse Core Ops, SparseCore 0:
  9.9 28.3 all-gather.7
  270.8 112.5 reduce-scatter.18
  385.3 28.4 all-gather.9
  415.4 28.1 all-gather.11
  445.7 64.5 all-gather.13
  527.3 111.5 reduce-scatter.22
  641.2 113.3 reduce-scatter.20
  759.2 65.0 all-gather.15
  937.4 111.5 reduce-scatter.24
  1051.9 34.6 reduce-scatter.38
  1090.4 46.2 reduce-scatter.26
  1138.8 134.0 reduce-scatter.34
  1275.2 130.3 reduce-scatter.36
  1409.4 47.6 reduce-scatter.30
  1461.2 51.3 reduce-scatter.32
  1516.1 35.9 reduce-scatter.28
